TPU v7x, 32 devices: a whole 2x2x4 slice. The times are simulated.
32 devices in a mesh: group: 1, expert: 16 (over z, y, x), step: 2 (over core).
Axes of the slice: x: 2, y: 2, z: 4, core: 2. Of those that a mesh axis runs over, the one named last changes fastest.
Arguments:
- latents: float32 [2, 2048, 1536], P('step', ('group', 'expert')), may hold values from -6 to 6
- modulation: float32 [2, 6, 1536], P('group'), may hold values from -3 to 3
- shallow_routes: int32 [2, 2048, 2], P('step', ('group', 'expert')), may hold values from 0 to 3, all different within a row; in each aligned block of 128 rows (0 to 127, 128 to 255, ..., all dimensions but the last counted through in order) at most 64 rows name the same one
- deep_routes: int32 [2048, 2], P(('group', 'expert')), may hold values from 0 to 3, all different within a row; in each aligned block of 128 rows (0 to 127, 128 to 255, ...) at most 64 rows name the same one
- refresh: int32 [16], P(('group', 'expert')), may hold values from 0 to 1
- shallow_in: bfloat16 [16, 1536, 768], P('expert'), may hold values from -0.15625 to 0.15625
- shallow_out: bfloat16 [16, 768, 1536], P('expert'), may hold values from -0.109375 to 0.109375
- deep_in: bfloat16 [16, 1536, 768], P('expert'), may hold values from -0.15625 to 0.15625
- deep_out: bfloat16 [16, 768, 1536], P('expert'), may hold values from -0.109375 to 0.109375
- shallow_router: float32 [1536, 4], replicated, may hold values from -0.15625 to 0.15625
- deep_router: float32 [1536, 4], replicated, may hold values from -0.15625 to 0.15625
Outputs:
- result: bfloat16 [2, 2048, 1536], P('step', ('group', 'expert'))
Inputs may be any that keep to these rules, and one draw needn't show every extreme that they name: `shallow_routes`: within the 128 rows of one index of expert (aligned blocks), each expert is named by at most 64 rows, and by exactly 64 rows in some block; a row names two different experts. `deep_routes`: within the 128 rows of one index of expert (aligned blocks), each expert is named by at most 64 rows, and by exactly 64 rows in some block; a row names two different experts.
All inputs are finite; a program needn't handle non-finite values.
Results may differ from a plain program's by a relative error of at most 0.01.
Values may be sent and summed in bfloat16 or wider, within the bound.
No kernel may reach another device: no remote copies, remote signals or barrier semaphores. Data moves between devices by JAX's collectives and lax.ppermute only.
A program may use at most 64 MiB of HBM per device.

v0:
```python
import jax
import jax.numpy as jnp
from jax import lax
from jax.sharding import PartitionSpec as P


def from_root(block, axis, owner):
    block = jnp.where(lax.axis_index(axis) == owner, block, jnp.zeros_like(block))
    return lax.psum(block, axis)


def modulate(hidden, shift_row, scale_row):
    average = jnp.mean(hidden, axis=-1, keepdims=True)
    centred = hidden - average
    variance = jnp.mean(centred * centred, axis=-1, keepdims=True)
    return (centred * lax.rsqrt(variance + 1e-06) * (1.0 + scale_row) + shift_row).astype(
        jnp.bfloat16
    )


def plan(normed, routes, router, capacity):
    rows_count, width = normed.shape
    experts = router.shape[1]
    logits = jnp.dot(normed.astype(jnp.float32), router, precision=lax.Precision.HIGHEST)
    hits = routes[:, :, None] == jnp.arange(experts, dtype=jnp.int32)
    chosen = jnp.sum(jnp.where(hits, logits[:, None, :], 0.0), axis=-1)
    gate_sig = jax.nn.sigmoid(chosen)
    weights = gate_sig / jnp.sum(gate_sig, axis=-1, keepdims=True)
    pair_hits = hits.reshape(rows_count * 2, experts).astype(jnp.int32)
    position = jnp.sum(pair_hits * (jnp.cumsum(pair_hits, axis=0) - 1), axis=-1).reshape(
        rows_count, 2
    )
    slot_hit = position[:, :, None] == jnp.arange(capacity, dtype=jnp.int32)
    placed = hits[:, :, :, None] & slot_hit[:, :, None, :]
    dispatch = jnp.any(placed, axis=1).reshape(rows_count, experts * capacity).astype(jnp.bfloat16)
    gathered = jnp.einsum("rs,rd->sd", dispatch, normed, preferred_element_type=jnp.float32).astype(
        jnp.bfloat16
    )
    combine_w = jnp.sum(jnp.where(placed, weights[:, :, None, None], 0.0), axis=1)
    return (gathered.reshape(experts, capacity, width), combine_w)


def spread(gathered, slices):
    experts, capacity, width = gathered.shape
    quarters = slices // experts
    return jnp.broadcast_to(gathered[:, None], (experts, quarters, capacity, width)).reshape(
        slices, capacity, width
    )


def expert_rows(piece, weight_in, weight_out):
    dims = piece.shape
    flat_rows = piece.reshape(-1, dims[-1])
    hidden = jax.nn.gelu(
        jnp.dot(flat_rows, weight_in, preferred_element_type=jnp.float32), approximate=True
    ).astype(jnp.bfloat16)
    return (
        jnp.dot(hidden, weight_out, preferred_element_type=jnp.float32)
        .astype(jnp.bfloat16)
        .reshape(dims)
    )


def combine(summed, combine_w):
    rows_count = combine_w.shape[0]
    width = summed.shape[-1]
    return jnp.dot(
        combine_w.reshape(rows_count, -1),
        summed.reshape(-1, width),
        precision=lax.Precision.HIGHEST,
        preferred_element_type=jnp.float32,
    )


def finish(returned, combine_w):
    experts = combine_w.shape[1]
    width = returned.shape[2]
    summed = jnp.sum(
        returned.astype(jnp.float32).reshape(experts, -1, returned.shape[1], width), axis=1
    )
    return combine(summed, combine_w)


def body(
    latents,
    modulation,
    shallow_routes,
    deep_routes,
    refresh,
    shallow_in,
    shallow_out,
    deep_in,
    deep_out,
    shallow_router,
    deep_router,
):
    slices = lax.axis_size("expert")
    experts = shallow_router.shape[1]
    rows_count = latents.shape[1]
    capacity = 2 * max(rows_count * 5 // 64, rows_count // experts)
    step_idx = lax.axis_index("step")
    root_idx = refresh[0]
    own_mod = lax.dynamic_index_in_dim(modulation, step_idx, 0, keepdims=False)
    features = latents[0]
    normed = modulate(features, own_mod[0], own_mod[1])
    gathered, combine_w = plan(normed, shallow_routes[0], shallow_router, capacity)
    partial_value = expert_rows(
        lax.all_to_all(spread(gathered, slices), "expert", split_axis=0, concat_axis=0, tiled=True),
        shallow_in[0],
        shallow_out[0],
    )
    returned = lax.all_to_all(partial_value, "expert", split_axis=0, concat_axis=0, tiled=True)
    moe_shallow = finish(returned, combine_w)
    after_shallow = (features + own_mod[2] * moe_shallow).astype(jnp.bfloat16)
    normed_deep = modulate(after_shallow.astype(jnp.float32), own_mod[3], own_mod[4])
    gathered_deep, combine_deep = plan(normed_deep, deep_routes, deep_router, capacity)
    partial_value = expert_rows(
        lax.all_to_all(
            spread(gathered_deep, slices), "expert", split_axis=0, concat_axis=0, tiled=True
        ),
        deep_in[0],
        deep_out[0],
    )
    returned_deep = lax.all_to_all(partial_value, "expert", split_axis=0, concat_axis=0, tiled=True)
    moe_deep = finish(returned_deep, combine_deep)
    own_delta = (own_mod[5] * moe_deep).astype(jnp.bfloat16)
    deep_delta = from_root(own_delta, "step", root_idx)
    result = (after_shallow.astype(jnp.float32) + deep_delta.astype(jnp.float32)).astype(
        jnp.bfloat16
    )
    return result[None]


def solution(mesh):
    in_specs = (
        P("step", ("group", "expert"), None),
        P("group", None, None),
        P("step", ("group", "expert"), None),
        P(("group", "expert"), None),
        P(("group", "expert")),
        P("expert", None, None),
        P("expert", None, None),
        P("expert", None, None),
        P("expert", None, None),
        P(),
        P(),
    )
    out_specs = P("step", ("group", "expert"), None)
    return jax.shard_map(body, mesh=mesh, in_specs=in_specs, out_specs=out_specs, check_vma=False)
```

profile of v0, /device:TPU:0, one launch (start us, length us, event | category | flops | bytes accessed | tf_op | source)
XLA Modules:
  0.0 376.2 jit_solution(6678324923360058093)
XLA Ops:
  6.5 0.9 copy.32
  7.6 0.1 eq.119
  7.8 1.3 reduce_sum.127
  9.0 1.4 multiply_reduce_fusion.1
  10.4 0.7 iota_compare_fusion.5
  11.1 1.2 reduce-window.14
  12.7 0.1 eq.127
  13.0 0.9 dynamic-slice_reduce_fusion.1
  13.9 1.6 convolution_convert_fusion.3
  15.6 0.3 broadcast_in_dim.82
  15.9 79.5 %all_to_all.20 = bf16[16,64,1536]{2,1,0:T(8,128)(2,1)} all-to-all(bf16[16,64,1536]{2,1,0:T(8,128)(2,1)S(1)} %bitcast.112), channel_id=1, replica_groups=mesh['group'=1,'expert'=16,'step'=2] {'expert'}, dimensions={0} | all-to-all | bytes 6291456 | tf_op jit(solution)/shard_map/all_to_all | solution.py:108
  95.4 10.4 %convolution_convert_fusion.1 = bf16[1024,1536]{1,0:T(8,128)(2,1)} fusion(bf16[1,768,1536]{2,1,0:T(8,128)(2,1)S(1)} %copy-done, bf16[1024,1536]{1,0:T(8,128)(2,1)} %bitcast.116, bf16[1,1536,768]{2,1,0:T(8,128)(2,1)} %param.16), kind=kOutput, calls=%fused_computation.5 | convolution fusion | flops 4840488960 | bytes 11010048 | tf_op jit(solution)/shard_map/dot_general | solution.py:58
  105.8 4.6 %all-to-all-start.1 = ((bf16[16,64,1536]{2,1,0:T(8,128)(2,1)}), bf16[16,64,1536]{2,1,0:T(8,128)(2,1)}, u32[]{:S(2)}, u32[]{:S(2)}) async-start(bf16[16,64,1536]{2,1,0:T(8,128)(2,1)} %bitcast.114), calls=%async_computation.1 | async-start | bytes 6291456 | tf_op jit(solution)/shard_map/all_to_all | solution.py:112
  110.7 0.1 eq.135
  110.9 1.2 reduce-window.16
  112.7 0.5 fusion.44
  113.5 57.2 %all-to-all-done.1 = bf16[16,64,1536]{2,1,0:T(8,128)(2,1)} async-done(((bf16[16,64,1536]{2,1,0:T(8,128)(2,1)}), bf16[16,64,1536]{2,1,0:T(8,128)(2,1)}, u32[]{:S(2)}, u32[]{:S(2)}) %all-to-all-start.1) | async-done | bytes 3145760 | tf_op jit(solution)/shard_map/all_to_all | solution.py:112
  170.7 2.6 convert_reduce_fusion.1
  173.2 1.1 fusion.61
  174.3 0.2 multiply_reduce_fusion
  174.6 0.2 add_convert_fusion.1
  174.8 0.3 convolution_convert_fusion.2
  175.2 0.3 broadcast_in_dim.86
  175.5 84.7 %all_to_all.21 = bf16[16,64,1536]{2,1,0:T(8,128)(2,1)} all-to-all(bf16[16,64,1536]{2,1,0:T(8,128)(2,1)S(1)} %bitcast.113), channel_id=1, replica_groups=mesh['group'=1,'expert'=16,'step'=2] {'expert'}, dimensions={0} | all-to-all | bytes 6291456 | tf_op jit(solution)/shard_map/all_to_all | solution.py:118
  260.3 11.1 %convolution_convert_fusion = bf16[1024,1536]{1,0:T(8,128)(2,1)} fusion(bf16[1,768,1536]{2,1,0:T(8,128)(2,1)} %param.19, bf16[1024,1536]{1,0:T(8,128)(2,1)} %bitcast.117, bf16[1,1536,768]{2,1,0:T(8,128)(2,1)} %param.18), kind=kOutput, calls=%fused_computation.4 | convolution fusion | flops 4840488960 | bytes 11010048 | tf_op jit(solution)/shard_map/dot_general | solution.py:58
  271.4 4.6 %all-to-all-start.3 = ((bf16[16,64,1536]{2,1,0:T(8,128)(2,1)}), bf16[16,64,1536]{2,1,0:T(8,128)(2,1)}, u32[]{:S(2)}, u32[]{:S(2)}) async-start(bf16[16,64,1536]{2,1,0:T(8,128)(2,1)} %bitcast.115), calls=%async_computation.3 | async-start | bytes 6291456 | tf_op jit(solution)/shard_map/all_to_all | solution.py:124
  276.7 0.4 fusion.62
  277.3 58.9 %all-to-all-done.3 = bf16[16,64,1536]{2,1,0:T(8,128)(2,1)} async-done(((bf16[16,64,1536]{2,1,0:T(8,128)(2,1)}), bf16[16,64,1536]{2,1,0:T(8,128)(2,1)}, u32[]{:S(2)}, u32[]{:S(2)}) %all-to-all-start.3) | async-done | bytes 3145760 | tf_op jit(solution)/shard_map/all_to_all | solution.py:124
  336.2 2.6 convert_reduce_fusion
  338.7 1.7 fusion.22
  340.5 27.0 %all-reduce.2.cloned.1.call-done = bf16[128,1536]{1,0:T(8,128)(2,1)} async-done(((bf16[128,1536]{1,0:T(8,128)(2,1)}), bf16[128,1536]{1,0:T(8,128)(2,1)}) %all-reduce.2.cloned.1.call-update) | async-done | bytes 393232 | tf_op jit(solution)/shard_map/psum | solution.py:9
  367.6 1.8 fusion.39
  (57 shorter events, 2.0 us)
Async XLA Ops:
  6.5 88.8 %copy-start = (bf16[1,768,1536]{2,1,0:T(8,128)(2,1)S(1)}, bf16[1,768,1536]{2,1,0:T(8,128)(2,1)}, u32[]{:S(2)}) copy-start(bf16[1,768,1536]{2,1,0:T(8,128)(2,1)} %param.17) | copy-start | bytes 7077892
  105.8 4.7 %copy-start.7 = (s32[128,2]{0,1:T(2,128)S(1)}, s32[128,2]{0,1:T(2,128)}, u32[]{:S(2)}) copy-start(s32[128,2]{0,1:T(2,128)} %param.14) | copy-start | bytes 3076
  105.8 6.9 %copy-start.1 = (f32[1,128,1536]{2,1,0:T(8,128)S(1)}, f32[1,128,1536]{2,1,0:T(8,128)}, u32[]{:S(2)}) copy-start(f32[1,128,1536]{2,1,0:T(8,128)} %param.11) | copy-start | bytes 2359300
  105.8 6.9 %copy-start.4 = (f32[1536,4]{0,1:T(4,128)S(1)}, f32[1536,4]{0,1:T(4,128)}, u32[]{:S(2)}) copy-start(f32[1536,4]{0,1:T(4,128)} %param.20) | copy-start | bytes 73732
  105.8 7.4 %copy-start.6 = (s32[1,128,2]{1,2,0:T(2,128)S(1)}, s32[1,128,2]{1,2,0:T(2,128)}, u32[]{:S(2)}) copy-start(s32[1,128,2]{1,2,0:T(2,128)} %param.13) | copy-start | bytes 3076
  105.8 64.8 %all-to-all-start.1 = ((bf16[16,64,1536]{2,1,0:T(8,128)(2,1)}), bf16[16,64,1536]{2,1,0:T(8,128)(2,1)}, u32[]{:S(2)}, u32[]{:S(2)}) async-start(bf16[16,64,1536]{2,1,0:T(8,128)(2,1)} %bitcast.114), calls=%async_computation.1 | async-start | bytes 6291456 | tf_op jit(solution)/shard_map/all_to_all | solution.py:112
  174.3 0.9 copy-start.2
  271.4 5.3 %copy-start.5 = (f32[1536,4]{0,1:T(4,128)S(1)}, f32[1536,4]{0,1:T(4,128)}, u32[]{:S(2)}) copy-start(f32[1536,4]{0,1:T(4,128)} %param.21) | copy-start | bytes 73732
  271.4 64.8 %all-to-all-start.3 = ((bf16[16,64,1536]{2,1,0:T(8,128)(2,1)}), bf16[16,64,1536]{2,1,0:T(8,128)(2,1)}, u32[]{:S(2)}, u32[]{:S(2)}) async-start(bf16[16,64,1536]{2,1,0:T(8,128)(2,1)} %bitcast.115), calls=%async_computation.3 | async-start | bytes 6291456 | tf_op jit(solution)/shard_map/all_to_all | solution.py:124
  276.0 91.6 %all-reduce.2.cloned.1.call-start = ((), (), s32[]{:S(2)}) async-start(), calls=%async_computation.4 | async-start | bytes 786432 | tf_op jit(solution)/shard_map/psum | solution.py:9
  277.3 90.3 %copy-start.3 = (f32[128,1536]{1,0:T(8,128)S(1)}, f32[128,1536]{1,0:T(8,128)}, u32[]{:S(2)}) copy-start(f32[128,1536]{1,0:T(8,128)} %copy-done.2) | copy-start | bytes 2359300
Sparse Core Ops, SparseCore 0:
  340.6 26.8 all-reduce.1
where the time goes:
time: 377 us; the launch traced here: 376 us
  blocking collectives  164 us (44%)
  waiting for transfers between devices  143 us (38%)
  matrix products  27.3 us (7%)
  other arithmetic  14.7 us (4%)
  between operations  14.3 us (4%)
  starting transfers between devices  9.3 us (2%)
    all_to_all x2, waiting for transfers between devices, body(): lax.all_to_all(partial_value, 'expert', split_axis=0, concat_axis=0, tile...  116 us
    all_to_all x1, blocking collectives, body(): lax.all_to_all(spread(gathered_deep, slices), 'expert', split_axis=0, con...  84.7 us
    all_to_all x1, blocking collectives, body(): lax.all_to_all(spread(gathered, slices), 'expert', split_axis=0, concat_a...  79.5 us
    psum x1, waiting for transfers between devices, from_root(): return lax.psum(block, axis)  27 us
    dot_general x2, matrix products, expert_rows(): jnp.dot(hidden, weight_out, preferred_element_type=jnp.float32)  21.5 us
    all_to_all x2, starting transfers between devices, body(): lax.all_to_all(partial_value, 'expert', split_axis=0, concat_axis=0, tile...  9.25 us
  transfers between devices with their start and end apart: 3, of which 3 were waited for; matrix products, arithmetic and copies ran while one was open for 1% of the time, Pallas kernels for 0%

commit v1 on v0

--- a/solution.py
+++ b/solution.py
@@ -114,12 +114,26 @@
     after_shallow = (features + own_mod[2] * moe_shallow).astype(jnp.bfloat16)
     normed_deep = modulate(after_shallow.astype(jnp.float32), own_mod[3], own_mod[4])
     gathered_deep, combine_deep = plan(normed_deep, deep_routes, deep_router, capacity)
+
+    def refer_frames(x_local, in_dim, dimension_no):
+        a_next, t_next = (lax.axis_size("expert"), lax.axis_index("expert"))
+        extra = x_local.shape[in_dim] // a_next
+        aux = jnp.roll(x_local, -t_next * extra, in_dim)
+        items = [lax.slice_in_dim(aux, 0, extra, axis=in_dim)]
+        for at in tuple(range(1, a_next)):
+            item_now = lax.slice_in_dim(aux, at * extra, (at + 1) * extra, axis=in_dim)
+            items.append(
+                lax.ppermute(item_now, "expert", [(pp, (pp + at) % a_next) for pp in range(a_next)])
+            )
+        next_value = jnp.roll(
+            jnp.concatenate(items[::-1], dimension_no),
+            shift=(t_next + 1) * items[0].shape[dimension_no],
+            axis=dimension_no,
+        )
+        return next_value
+
     partial_value = expert_rows(
-        lax.all_to_all(
-            spread(gathered_deep, slices), "expert", split_axis=0, concat_axis=0, tiled=True
-        ),
-        deep_in[0],
-        deep_out[0],
+        refer_frames(spread(gathered_deep, slices), 0, 0), deep_in[0], deep_out[0]
     )
     returned_deep = lax.all_to_all(partial_value, "expert", split_axis=0, concat_axis=0, tiled=True)
     moe_deep = finish(returned_deep, combine_deep)

time: 377 us -> 417 us (1.11)
  blocking collectives: 164 us -> 79.5 us
  starting transfers between devices: 9.3 us -> 73 us
  waiting for transfers between devices: 143 us -> 193 us
  local copies, waits for them, and re-layouts: 3.26 us -> 9.5 us
  other arithmetic: 14.7 us -> 19.2 us
    all_to_all x1 -> x0, blocking collectives: 84.7 us -> none  [body(): lax.all_to_all(spread(gathered_deep, slices), 'expert', split_axis=0, con...]
    ppermute x0 -> x15, starting transfers between devices: none -> 63.7 us  [refer_frames(): lax.ppermute(item_now, 'expert', [(pp, (pp + at) % a_next) for pp in rang...]
    ppermute x0 -> x15, waiting for transfers between devices: none -> 54.9 us  [refer_frames(): lax.ppermute(item_now, 'expert', [(pp, (pp + at) % a_next) for pp in rang...]
  transfers between devices with their start and end apart: 3 -> 18, of which waited for: 3 -> 13; matrix products, arithmetic and copies ran while one was open for 1% -> 1% of each run, Pallas kernels for 0% -> 0%
where the time goes in v1:
time: 417 us; the launch traced here: 416 us
  waiting for transfers between devices  193 us (46%)
  blocking collectives  79.5 us (19%)
  starting transfers between devices  73 us (18%)
  matrix products  27.3 us (7%)
  other arithmetic  19.2 us (5%)
  between operations  14.5 us (3%)
  local copies, waits for them, and re-layouts  9.5 us (2%)
    all_to_all x2, waiting for transfers between devices, body(): lax.all_to_all(partial_value, 'expert', split_axis=0, concat_axis=0, tile...  112 us
    all_to_all x1, blocking collectives, body(): lax.all_to_all(spread(gathered, slices), 'expert', split_axis=0, concat_a...  79.5 us
    ppermute x15, starting transfers between devices, refer_frames(): lax.ppermute(item_now, 'expert', [(pp, (pp + at) % a_next) for pp in rang...  63.7 us
    ppermute x15, waiting for transfers between devices, refer_frames(): lax.ppermute(item_now, 'expert', [(pp, (pp + at) % a_next) for pp in rang...  54.9 us
    psum x1, waiting for transfers between devices, from_root(): return lax.psum(block, axis)  26.3 us
    dot_general x2, matrix products, expert_rows(): jnp.dot(hidden, weight_out, preferred_element_type=jnp.float32)  21.5 us
    all_to_all x2, starting transfers between devices, body(): lax.all_to_all(partial_value, 'expert', split_axis=0, concat_axis=0, tile...  9.25 us
  transfers between devices with their start and end apart: 18, of which 13 were waited for; matrix products, arithmetic and copies ran while one was open for 1% of the time, Pallas kernels for 0%

profile of v1, /device:TPU:0, one launch (start us, length us, event | category | flops | bytes accessed | tf_op | source)
XLA Modules:
  0.0 416.4 jit_solution(5347170742602002612)
XLA Ops:
  19.1 79.5 %all_to_all.15 = bf16[16,64,1536]{2,1,0:T(8,128)(2,1)} all-to-all(bf16[16,64,1536]{2,1,0:T(8,128)(2,1)S(1)} %bitcast.113), channel_id=1, replica_groups=mesh['group'=1,'expert'=16,'step'=2] {'expert'}, dimensions={0} | all-to-all | bytes 6291456 | tf_op jit(solution)/shard_map/all_to_all | solution.py:108
  98.7 10.4 %convolution_convert_fusion.1 = bf16[1024,1536]{1,0:T(8,128)(2,1)} fusion(bf16[1,768,1536]{2,1,0:T(8,128)(2,1)S(1)} %copy-done, bf16[1024,1536]{1,0:T(8,128)(2,1)} %bitcast.117, bf16[1,1536,768]{2,1,0:T(8,128)(2,1)} %param.18), kind=kOutput, calls=%fused_computation.9 | convolution fusion | flops 4840488960 | bytes 11010048 | tf_op jit(solution)/shard_map/dot_general | solution.py:58
  109.1 4.6 %all-to-all-start.1 = ((bf16[16,64,1536]{2,1,0:T(8,128)(2,1)}), bf16[16,64,1536]{2,1,0:T(8,128)(2,1)}, u32[]{:S(2)}, u32[]{:S(2)}) async-start(bf16[16,64,1536]{2,1,0:T(8,128)(2,1)} %bitcast.114), calls=%async_computation.1 | async-start | bytes 6291456 | tf_op jit(solution)/shard_map/all_to_all | solution.py:112
  115.2 58.8 %all-to-all-done.1 = bf16[16,64,1536]{2,1,0:T(8,128)(2,1)} async-done(((bf16[16,64,1536]{2,1,0:T(8,128)(2,1)}), bf16[16,64,1536]{2,1,0:T(8,128)(2,1)}, u32[]{:S(2)}, u32[]{:S(2)}) %all-to-all-start.1) | async-done | bytes 3145760 | tf_op jit(solution)/shard_map/all_to_all | solution.py:112
  173.9 2.6 convert_reduce_fusion.1
  182.9 12.5 %collective-permute-start = (bf16[1,64,1536]{2,1,0:T(8,128)(2,1)}, bf16[1,64,1536]{2,1,0:T(8,128)(2,1)}, u32[]{:S(2)}, u32[]{:S(2)}) collective-permute-start(bf16[1,64,1536]{2,1,0:T(8,128)(2,1)} %get-tuple-element.26), channel_id=1, source_target_pairs={{0,30},{2,0},{4,2},{6,4},{8,6},{10,8},{12,10},{14,12},{16,14},{18,... | collective-permute-start | bytes 589832 | tf_op jit(solution)/shard_map/ppermute | solution.py:126
  195.5 2.6 collective-permute-start.12
  200.1 4.7 %collective-permute-start.1 = (bf16[1,64,1536]{2,1,0:T(8,128)(2,1)}, bf16[1,64,1536]{2,1,0:T(8,128)(2,1)S(1)}, u32[]{:S(2)}, u32[]{:S(2)}) collective-permute-start(bf16[1,64,1536]{2,1,0:T(8,128)(2,1)} %get-tuple-element.25), channel_id=1, source_target_pairs={{0,28},{2,30},{4,0},{6,2},{8,4},{10,6},{12,8},{14,10},{16,12},{18,... | collective-permute-start | bytes 589832 | tf_op jit(solution)/shard_map/ppermute | solution.py:126
  205.7 4.7 %collective-permute-done.1 = bf16[1,64,1536]{2,1,0:T(8,128)(2,1)S(1)} collective-permute-done((bf16[1,64,1536]{2,1,0:T(8,128)(2,1)}, bf16[1,64,1536]{2,1,0:T(8,128)(2,1)S(1)}, u32[]{:S(2)}, u32[]{:S(2)}) %collective-permute-start.1) | collective-permute-done | bytes 196640 | tf_op jit(solution)/shard_map/ppermute | solution.py:126
  210.4 4.0 collective-permute-start.2
  214.5 4.6 %collective-permute-done.2 = bf16[1,64,1536]{2,1,0:T(8,128)(2,1)S(1)} collective-permute-done((bf16[1,64,1536]{2,1,0:T(8,128)(2,1)}, bf16[1,64,1536]{2,1,0:T(8,128)(2,1)S(1)}, u32[]{:S(2)}, u32[]{:S(2)}) %collective-permute-start.2) | collective-permute-done | bytes 196640 | tf_op jit(solution)/shard_map/ppermute | solution.py:126
  219.1 2.4 collective-permute-start.3
  221.5 3.8 collective-permute-done.3
  225.2 3.2 collective-permute-start.4
  228.5 3.6 collective-permute-done.4
  232.0 3.6 collective-permute-start.5
  235.6 3.6 collective-permute-done.5
  239.2 12.3 %collective-permute-start.6 = (bf16[1,64,1536]{2,1,0:T(8,128)(2,1)}, bf16[1,64,1536]{2,1,0:T(8,128)(2,1)S(1)}, u32[]{:S(2)}, u32[]{:S(2)}) collective-permute-start(bf16[1,64,1536]{2,1,0:T(8,128)(2,1)} %get-tuple-element.20), channel_id=1, source_target_pairs={{0,18},{2,20},{4,22},{6,24},{8,26},{10,28},{12,30},{14,0},{16,2},{... | collective-permute-start | bytes 589832 | tf_op jit(solution)/shard_map/ppermute | solution.py:126
  251.6 4.8 %collective-permute-done.6 = bf16[1,64,1536]{2,1,0:T(8,128)(2,1)S(1)} collective-permute-done((bf16[1,64,1536]{2,1,0:T(8,128)(2,1)}, bf16[1,64,1536]{2,1,0:T(8,128)(2,1)S(1)}, u32[]{:S(2)}, u32[]{:S(2)}) %collective-permute-start.6) | collective-permute-done | bytes 196640 | tf_op jit(solution)/shard_map/ppermute | solution.py:126
  256.4 7.1 %collective-permute-start.7 = (bf16[1,64,1536]{2,1,0:T(8,128)(2,1)}, bf16[1,64,1536]{2,1,0:T(8,128)(2,1)S(1)}, u32[]{:S(2)}, u32[]{:S(2)}) collective-permute-start(bf16[1,64,1536]{2,1,0:T(8,128)(2,1)} %get-tuple-element.19), channel_id=1, source_target_pairs={{0,16},{2,18},{4,20},{6,22},{8,24},{10,26},{12,28},{14,30},{16,0},... | collective-permute-start | bytes 589832 | tf_op jit(solution)/shard_map/ppermute | solution.py:126
  263.5 5.5 %collective-permute-done.7 = bf16[1,64,1536]{2,1,0:T(8,128)(2,1)S(1)} collective-permute-done((bf16[1,64,1536]{2,1,0:T(8,128)(2,1)}, bf16[1,64,1536]{2,1,0:T(8,128)(2,1)S(1)}, u32[]{:S(2)}, u32[]{:S(2)}) %collective-permute-start.7) | collective-permute-done | bytes 196640 | tf_op jit(solution)/shard_map/ppermute | solution.py:126
  269.0 6.0 %collective-permute-start.8 = (bf16[1,64,1536]{2,1,0:T(8,128)(2,1)}, bf16[1,64,1536]{2,1,0:T(8,128)(2,1)S(1)}, u32[]{:S(2)}, u32[]{:S(2)}) collective-permute-start(bf16[1,64,1536]{2,1,0:T(8,128)(2,1)} %get-tuple-element.18), channel_id=1, source_target_pairs={{0,14},{2,16},{4,18},{6,20},{8,22},{10,24},{12,26},{14,28},{16,30}... | collective-permute-start | bytes 589832 | tf_op jit(solution)/shard_map/ppermute | solution.py:126
  275.1 5.5 %collective-permute-done.8 = bf16[1,64,1536]{2,1,0:T(8,128)(2,1)S(1)} collective-permute-done((bf16[1,64,1536]{2,1,0:T(8,128)(2,1)}, bf16[1,64,1536]{2,1,0:T(8,128)(2,1)S(1)}, u32[]{:S(2)}, u32[]{:S(2)}) %collective-permute-start.8) | collective-permute-done | bytes 196640 | tf_op jit(solution)/shard_map/ppermute | solution.py:126
  280.6 3.2 collective-permute-start.9
  283.8 8.5 %collective-permute-done.9 = bf16[1,64,1536]{2,1,0:T(8,128)(2,1)S(1)} collective-permute-done((bf16[1,64,1536]{2,1,0:T(8,128)(2,1)S(1)}, bf16[1,64,1536]{2,1,0:T(8,128)(2,1)S(1)}, u32[]{:S(2)}, u32[]{:S(2)}) %collective-permute-start.9) | collective-permute-done | bytes 196640 | tf_op jit(solution)/shard_map/ppermute | solution.py:126
  292.3 10.3 %collective-permute-done.10 = bf16[1,64,1536]{2,1,0:T(8,128)(2,1)S(1)} collective-permute-done((bf16[1,64,1536]{2,1,0:T(8,128)(2,1)S(1)}, bf16[1,64,1536]{2,1,0:T(8,128)(2,1)S(1)}, u32[]{:S(2)}, u32[]{:S(2)}) %collective-permute-start.10) | collective-permute-done | bytes 196640 | tf_op jit(solution)/shard_map/ppermute | solution.py:126
  303.7 2.8 fusion.16
  306.6 11.1 %convolution_convert_fusion = bf16[1024,1536]{1,0:T(8,128)(2,1)} fusion(bf16[1,768,1536]{2,1,0:T(8,128)(2,1)} %param.21, bf16[1024,1536]{1,0:T(8,128)(2,1)} %bitcast.116, bf16[1,1536,768]{2,1,0:T(8,128)(2,1)} %param.20), kind=kOutput, calls=%fused_computation.8 | convolution fusion | flops 4840488960 | bytes 11010048 | tf_op jit(solution)/shard_map/dot_general | solution.py:58
  317.7 4.6 %all-to-all-start.2 = ((bf16[16,64,1536]{2,1,0:T(8,128)(2,1)}), bf16[16,64,1536]{2,1,0:T(8,128)(2,1)}, u32[]{:S(2)}, u32[]{:S(2)}) async-start(bf16[16,64,1536]{2,1,0:T(8,128)(2,1)} %bitcast.115), calls=%async_computation.2 | async-start | bytes 6291456 | tf_op jit(solution)/shard_map/all_to_all | solution.py:138
  323.6 53.5 %all-to-all-done.2 = bf16[16,64,1536]{2,1,0:T(8,128)(2,1)} async-done(((bf16[16,64,1536]{2,1,0:T(8,128)(2,1)}), bf16[16,64,1536]{2,1,0:T(8,128)(2,1)}, u32[]{:S(2)}, u32[]{:S(2)}) %all-to-all-start.2) | async-done | bytes 3145760 | tf_op jit(solution)/shard_map/all_to_all | solution.py:138
  377.1 2.6 convert_reduce_fusion
  381.5 26.3 %all-reduce.2.cloned.1.call-done = bf16[128,1536]{1,0:T(8,128)(2,1)} async-done(((bf16[128,1536]{1,0:T(8,128)(2,1)}), bf16[128,1536]{1,0:T(8,128)(2,1)}) %all-reduce.2.cloned.1.call-update) | async-done | bytes 393232 | tf_op jit(solution)/shard_map/psum | solution.py:9
  (118 shorter events, 28.6 us)
Async XLA Ops:
  6.5 92.1 %copy-start = (bf16[1,768,1536]{2,1,0:T(8,128)(2,1)S(1)}, bf16[1,768,1536]{2,1,0:T(8,128)(2,1)}, u32[]{:S(2)}) copy-start(bf16[1,768,1536]{2,1,0:T(8,128)(2,1)} %param.19) | copy-start | bytes 7077892
  109.1 4.9 %copy-start.1 = (f32[1,128,1536]{2,1,0:T(8,128)S(1)}, f32[1,128,1536]{2,1,0:T(8,128)}, u32[]{:S(2)}) copy-start(f32[1,128,1536]{2,1,0:T(8,128)} %param.13) | copy-start | bytes 2359300
  109.1 4.9 %copy-start.8 = (f32[1536,4]{0,1:T(4,128)S(1)}, f32[1536,4]{0,1:T(4,128)}, u32[]{:S(2)}) copy-start(f32[1536,4]{0,1:T(4,128)} %param.22) | copy-start | bytes 73732
  109.1 5.4 %copy-start.12 = (s32[1,128,2]{1,2,0:T(2,128)S(1)}, s32[1,128,2]{1,2,0:T(2,128)}, u32[]{:S(2)}) copy-start(s32[1,128,2]{1,2,0:T(2,128)} %param.15) | copy-start | bytes 3076
  109.1 5.5 %copy-start.13 = (s32[128,2]{0,1:T(2,128)S(1)}, s32[128,2]{0,1:T(2,128)}, u32[]{:S(2)}) copy-start(s32[128,2]{0,1:T(2,128)} %param.16) | copy-start | bytes 3076
  109.1 64.8 %all-to-all-start.1 = ((bf16[16,64,1536]{2,1,0:T(8,128)(2,1)}), bf16[16,64,1536]{2,1,0:T(8,128)(2,1)}, u32[]{:S(2)}, u32[]{:S(2)}) async-start(bf16[16,64,1536]{2,1,0:T(8,128)(2,1)} %bitcast.114), calls=%async_computation.1 | async-start | bytes 6291456 | tf_op jit(solution)/shard_map/all_to_all | solution.py:112
  177.6 0.9 copy-start.3
  179.9 1.7 copy-start.2
  182.9 17.1 %collective-permute-start = (bf16[1,64,1536]{2,1,0:T(8,128)(2,1)}, bf16[1,64,1536]{2,1,0:T(8,128)(2,1)}, u32[]{:S(2)}, u32[]{:S(2)}) collective-permute-start(bf16[1,64,1536]{2,1,0:T(8,128)(2,1)} %get-tuple-element.26), channel_id=1, source_target_pairs={{0,30},{2,0},{4,2},{6,4},{8,6},{10,8},{12,10},{14,12},{16,14},{18,... | collective-permute-start | bytes 589832 | tf_op jit(solution)/shard_map/ppermute | solution.py:126
  195.4 85.1 %copy-start.6 = (bf16[1,64,1536]{2,1,0:T(8,128)(2,1)S(1)}, bf16[1,64,1536]{2,1,0:T(8,128)(2,1)}, u32[]{:S(2)}) copy-start(bf16[1,64,1536]{2,1,0:T(8,128)(2,1)} %get-tuple-element.17) | copy-start | bytes 589828
  195.5 96.9 %copy-start.5 = (bf16[1,64,1536]{2,1,0:T(8,128)(2,1)S(1)}, bf16[1,64,1536]{2,1,0:T(8,128)(2,1)}, u32[]{:S(2)}) copy-start(bf16[1,64,1536]{2,1,0:T(8,128)(2,1)} %get-tuple-element.16) | copy-start | bytes 589828
  195.5 107.3 %collective-permute-start.14 = (bf16[1,64,1536]{2,1,0:T(8,128)(2,1)S(1)}, bf16[1,64,1536]{2,1,0:T(8,128)(2,1)S(1)}, u32[]{:S(2)}, u32[]{:S(2)}) collective-permute-start(bf16[1,64,1536]{2,1,0:T(8,128)(2,1)S(1)} %get-tuple-element.12), channel_id=1, source_target_pairs={{0,2},{2,4},{4,6},{6,8},{8,10},{10,12},{12,14},{14,16},{16,18},{18... | collective-permute-start | bytes 589832 | tf_op jit(solution)/shard_map/ppermute | solution.py:126
  195.5 107.2 %collective-permute-start.13 = (bf16[1,64,1536]{2,1,0:T(8,128)(2,1)S(1)}, bf16[1,64,1536]{2,1,0:T(8,128)(2,1)S(1)}, u32[]{:S(2)}, u32[]{:S(2)}) collective-permute-start(bf16[1,64,1536]{2,1,0:T(8,128)(2,1)S(1)} %get-tuple-element.13), channel_id=1, source_target_pairs={{0,4},{2,6},{4,8},{6,10},{8,12},{10,14},{12,16},{14,18},{16,20},{1... | collective-permute-start | bytes 589832 | tf_op jit(solution)/shard_map/ppermute | solution.py:126
  195.5 107.2 %collective-permute-start.12 = (bf16[1,64,1536]{2,1,0:T(8,128)(2,1)S(1)}, bf16[1,64,1536]{2,1,0:T(8,128)(2,1)S(1)}, u32[]{:S(2)}, u32[]{:S(2)}) collective-permute-start(bf16[1,64,1536]{2,1,0:T(8,128)(2,1)S(1)} %get-tuple-element.14), channel_id=1, source_target_pairs={{0,6},{2,8},{4,10},{6,12},{8,14},{10,16},{12,18},{14,20},{16,22},{... | collective-permute-start | bytes 589832 | tf_op jit(solution)/shard_map/ppermute | solution.py:126
  198.1 104.6 %collective-permute-start.11 = (bf16[1,64,1536]{2,1,0:T(8,128)(2,1)S(1)}, bf16[1,64,1536]{2,1,0:T(8,128)(2,1)S(1)}, u32[]{:S(2)}, u32[]{:S(2)}) collective-permute-start(bf16[1,64,1536]{2,1,0:T(8,128)(2,1)S(1)} %get-tuple-element.15), channel_id=1, source_target_pairs={{0,8},{2,10},{4,12},{6,14},{8,16},{10,18},{12,20},{14,22},{16,24},... | collective-permute-start | bytes 589832 | tf_op jit(solution)/shard_map/ppermute | solution.py:126
  200.1 10.3 %collective-permute-start.1 = (bf16[1,64,1536]{2,1,0:T(8,128)(2,1)}, bf16[1,64,1536]{2,1,0:T(8,128)(2,1)S(1)}, u32[]{:S(2)}, u32[]{:S(2)}) collective-permute-start(bf16[1,64,1536]{2,1,0:T(8,128)(2,1)} %get-tuple-element.25), channel_id=1, source_target_pairs={{0,28},{2,30},{4,0},{6,2},{8,4},{10,6},{12,8},{14,10},{16,12},{18,... | collective-permute-start | bytes 589832 | tf_op jit(solution)/shard_map/ppermute | solution.py:126
  210.4 8.7 %collective-permute-start.2 = (bf16[1,64,1536]{2,1,0:T(8,128)(2,1)}, bf16[1,64,1536]{2,1,0:T(8,128)(2,1)S(1)}, u32[]{:S(2)}, u32[]{:S(2)}) collective-permute-start(bf16[1,64,1536]{2,1,0:T(8,128)(2,1)} %get-tuple-element.24), channel_id=1, source_target_pairs={{0,26},{2,28},{4,30},{6,0},{8,2},{10,4},{12,6},{14,8},{16,10},{18,... | collective-permute-start | bytes 589832 | tf_op jit(solution)/shard_map/ppermute | solution.py:126
  219.1 6.2 %collective-permute-start.3 = (bf16[1,64,1536]{2,1,0:T(8,128)(2,1)}, bf16[1,64,1536]{2,1,0:T(8,128)(2,1)S(1)}, u32[]{:S(2)}, u32[]{:S(2)}) collective-permute-start(bf16[1,64,1536]{2,1,0:T(8,128)(2,1)} %get-tuple-element.23), channel_id=1, source_target_pairs={{0,24},{2,26},{4,28},{6,30},{8,0},{10,2},{12,4},{14,6},{16,8},{18,... | collective-permute-start | bytes 589832 | tf_op jit(solution)/shard_map/ppermute | solution.py:126
  225.2 6.8 %collective-permute-start.4 = (bf16[1,64,1536]{2,1,0:T(8,128)(2,1)}, bf16[1,64,1536]{2,1,0:T(8,128)(2,1)S(1)}, u32[]{:S(2)}, u32[]{:S(2)}) collective-permute-start(bf16[1,64,1536]{2,1,0:T(8,128)(2,1)} %get-tuple-element.22), channel_id=1, source_target_pairs={{0,22},{2,24},{4,26},{6,28},{8,30},{10,0},{12,2},{14,4},{16,6},{18... | collective-permute-start | bytes 589832 | tf_op jit(solution)/shard_map/ppermute | solution.py:126
  232.0 7.2 %collective-permute-start.5 = (bf16[1,64,1536]{2,1,0:T(8,128)(2,1)}, bf16[1,64,1536]{2,1,0:T(8,128)(2,1)S(1)}, u32[]{:S(2)}, u32[]{:S(2)}) collective-permute-start(bf16[1,64,1536]{2,1,0:T(8,128)(2,1)} %get-tuple-element.21), channel_id=1, source_target_pairs={{0,20},{2,22},{4,24},{6,26},{8,28},{10,30},{12,0},{14,2},{16,4},{1... | collective-permute-start | bytes 589832 | tf_op jit(solution)/shard_map/ppermute | solution.py:126
  239.2 17.2 %collective-permute-start.6 = (bf16[1,64,1536]{2,1,0:T(8,128)(2,1)}, bf16[1,64,1536]{2,1,0:T(8,128)(2,1)S(1)}, u32[]{:S(2)}, u32[]{:S(2)}) collective-permute-start(bf16[1,64,1536]{2,1,0:T(8,128)(2,1)} %get-tuple-element.20), channel_id=1, source_target_pairs={{0,18},{2,20},{4,22},{6,24},{8,26},{10,28},{12,30},{14,0},{16,2},{... | collective-permute-start | bytes 589832 | tf_op jit(solution)/shard_map/ppermute | solution.py:126
  256.4 12.6 %collective-permute-start.7 = (bf16[1,64,1536]{2,1,0:T(8,128)(2,1)}, bf16[1,64,1536]{2,1,0:T(8,128)(2,1)S(1)}, u32[]{:S(2)}, u32[]{:S(2)}) collective-permute-start(bf16[1,64,1536]{2,1,0:T(8,128)(2,1)} %get-tuple-element.19), channel_id=1, source_target_pairs={{0,16},{2,18},{4,20},{6,22},{8,24},{10,26},{12,28},{14,30},{16,0},... | collective-permute-start | bytes 589832 | tf_op jit(solution)/shard_map/ppermute | solution.py:126
  269.0 11.6 %collective-permute-start.8 = (bf16[1,64,1536]{2,1,0:T(8,128)(2,1)}, bf16[1,64,1536]{2,1,0:T(8,128)(2,1)S(1)}, u32[]{:S(2)}, u32[]{:S(2)}) collective-permute-start(bf16[1,64,1536]{2,1,0:T(8,128)(2,1)} %get-tuple-element.18), channel_id=1, source_target_pairs={{0,14},{2,16},{4,18},{6,20},{8,22},{10,24},{12,26},{14,28},{16,30}... | collective-permute-start | bytes 589832 | tf_op jit(solution)/shard_map/ppermute | solution.py:126
  280.6 11.7 %collective-permute-start.9 = (bf16[1,64,1536]{2,1,0:T(8,128)(2,1)S(1)}, bf16[1,64,1536]{2,1,0:T(8,128)(2,1)S(1)}, u32[]{:S(2)}, u32[]{:S(2)}) collective-permute-start(bf16[1,64,1536]{2,1,0:T(8,128)(2,1)S(1)} %copy-done.6), channel_id=1, source_target_pairs={{0,12},{2,14},{4,16},{6,18},{8,20},{10,22},{12,24},{14,26},{16,28}... | collective-permute-start | bytes 589832 | tf_op jit(solution)/shard_map/ppermute | solution.py:126
  292.3 10.3 %collective-permute-start.10 = (bf16[1,64,1536]{2,1,0:T(8,128)(2,1)S(1)}, bf16[1,64,1536]{2,1,0:T(8,128)(2,1)S(1)}, u32[]{:S(2)}, u32[]{:S(2)}) collective-permute-start(bf16[1,64,1536]{2,1,0:T(8,128)(2,1)S(1)} %copy-done.5), channel_id=1, source_target_pairs={{0,10},{2,12},{4,14},{6,16},{8,18},{10,20},{12,22},{14,24},{16,26}... | collective-permute-start | bytes 589832 | tf_op jit(solution)/shard_map/ppermute | solution.py:126
  317.7 5.3 %copy-start.9 = (f32[1536,4]{0,1:T(4,128)S(1)}, f32[1536,4]{0,1:T(4,128)}, u32[]{:S(2)}) copy-start(f32[1536,4]{0,1:T(4,128)} %param.23) | copy-start | bytes 73732
  317.7 5.7 %copy-start.14 = (s32[128,2]{0,1:T(2,128)S(1)}, s32[128,2]{0,1:T(2,128)}, u32[]{:S(2)}) copy-start(s32[128,2]{0,1:T(2,128)} %param.16) | copy-start | bytes 3076
  317.7 5.8 %copy-start.11 = (pred[128,2,4]{0,2,1:T(4,128)(4,1)S(1)}, pred[128,2,4]{0,2,1:T(4,128)(4,1)}, u32[]{:S(2)}) copy-start(pred[128,2,4]{0,2,1:T(4,128)(4,1)} %copy-done.10) | copy-start | bytes 3076
  317.7 59.4 %all-to-all-start.2 = ((bf16[16,64,1536]{2,1,0:T(8,128)(2,1)}), bf16[16,64,1536]{2,1,0:T(8,128)(2,1)}, u32[]{:S(2)}, u32[]{:S(2)}) async-start(bf16[16,64,1536]{2,1,0:T(8,128)(2,1)} %bitcast.115), calls=%async_computation.2 | async-start | bytes 6291456 | tf_op jit(solution)/shard_map/all_to_all | solution.py:138
  322.3 57.4 %copy-start.7 = (f32[1536]{0:T(1024)S(1)}, f32[1536]{0:T(1024)}, u32[]{:S(2)}) copy-start(f32[1536]{0:T(1024)} %get-tuple-element.6) | copy-start | bytes 18436
  322.3 85.4 %all-reduce.2.cloned.1.call-start = ((), (), s32[]{:S(2)}) async-start(), calls=%async_computation.3 | async-start | bytes 786432 | tf_op jit(solution)/shard_map/psum | solution.py:9
  323.6 84.2 %copy-start.4 = (f32[128,1536]{1,0:T(8,128)S(1)}, f32[128,1536]{1,0:T(8,128)}, u32[]{:S(2)}) copy-start(f32[128,1536]{1,0:T(8,128)} %copy-done.3) | copy-start | bytes 2359300
  (1 other events, 0.5 us)
Sparse Core Ops, SparseCore 0:
  381.6 26.1 all-reduce.1
